TPU v7x, 32 devices: a whole 2x2x4 slice. The times are simulated.
32 devices in a mesh: dp: 2 (over x), cols: 16 (over z, y, core).
Axes of the slice: x: 2, y: 2, z: 4, core: 2. Of those that a mesh axis runs over, the one named last changes fastest.
Arguments:
- tokens: bfloat16 [512, 4096], P(('dp', 'cols')), may hold values from -6 to 6
- cotangent: bfloat16 [512, 4096], P(('dp', 'cols')), may hold values from -6 to 6
- block_weights: bfloat16 [4096, 128, 128], P('cols'), may hold values from -0.15625 to 0.15625
- slot_block: int32 [4096], P('cols'), may hold values from 0 to 31
- slot_target: int32 [4096], P('cols'), may hold values from 0 to 23, as said below
- counts: int32 [16], P('cols'), may hold values from 171 to 256, as said below
Outputs:
- input_grad: bfloat16 [512, 4096], P(('dp', 'cols'))
- weight_grad: bfloat16 [4096, 128, 128], P('cols', 'dp')
Inputs may be any that keep to these rules, and one draw needn't show every extreme that they name: On each device the live slots name distinct pairs of slot_target and slot_block; slot_target // 8 gives the matrix (0 gate, 1 up, 2 down). `counts`: some device has all 256 slots live.
All inputs are finite; a program needn't handle non-finite values.
Results may differ from a plain program's by a relative error of at most 0.018.
Values may be sent and summed in bfloat16 or wider, within the bound.
A program may use at most 192 MiB of HBM per device.

v0:
```python
import jax
import jax.numpy as jnp
from jax import lax
from jax.sharding import PartitionSpec as P

SPC = 32


def block_inputs(grad_rows, weights, block_select):
    partial_rows = jnp.einsum(
        "rsj,skj->rsk", grad_rows, weights, preferred_element_type=jnp.float32
    )
    summed = jnp.einsum("rsk,sb->rbk", partial_rows, block_select)
    return summed.reshape(summed.shape[0], summed.shape[1] * summed.shape[2])


def shards(tokens, cotangent, block_weights, slot_block, slot_target, counts):
    slot_total = block_weights.shape[0]
    block_width = block_weights.shape[1]
    columns = slot_total // SPC
    features = tokens.shape[1]
    block_count = features // block_width
    tokens_all, cot_all = (
        lax.all_gather(tokens, "cols", axis=0, tiled=True),
        lax.all_gather(cotangent, "cols", axis=0, tiled=True),
    )
    row_total = tokens_all.shape[0]
    live_slot = jnp.arange(slot_total) < counts[0]
    slot_kind = slot_target // columns
    places = slot_target % columns
    up_mask = (live_slot & (slot_kind < 2))[:, None].astype(jnp.float32)
    down_mask = (live_slot & (slot_kind == 2))[:, None].astype(jnp.float32)
    select_up = jax.nn.one_hot(slot_target, 2 * columns, dtype=jnp.float32) * up_mask
    select_down = jax.nn.one_hot(places, columns, dtype=jnp.float32) * down_mask
    block_select = jax.nn.one_hot(slot_block, block_count, dtype=jnp.float32)
    tokens_slots = jnp.take(
        tokens_all.reshape(row_total, block_count, block_width), slot_block, axis=1
    )
    products = jnp.einsum(
        "rsk,skj->rsj", tokens_slots, block_weights, preferred_element_type=jnp.float32
    )
    gate_up = jnp.einsum("rsj,sc->rcj", products, select_up)
    gate_pre = gate_up[:, :columns]
    up_pre = gate_up[:, columns:]
    sigmoid_gate = jax.nn.sigmoid(gate_pre)
    silu_gate = gate_pre * sigmoid_gate
    hidden = (silu_gate * up_pre).astype(jnp.bfloat16)
    cot_slots = jnp.take(cot_all.reshape(row_total, block_count, block_width), slot_block, axis=1)
    back_products = jnp.einsum(
        "rsj,skj->rsk", cot_slots, block_weights, preferred_element_type=jnp.float32
    )
    hidden_grad = jnp.einsum("rsk,sc->rck", back_products, select_down)
    gate_grad = (
        hidden_grad * up_pre * sigmoid_gate * (1.0 + gate_pre * (1.0 - sigmoid_gate))
    ).astype(jnp.bfloat16)
    up_grad = (hidden_grad * silu_gate).astype(jnp.bfloat16)
    pre_grad = jnp.concatenate([gate_grad, up_grad], axis=1)
    slot_grad = jnp.einsum(
        "rck,sc->rsk", pre_grad, select_up.astype(jnp.bfloat16), preferred_element_type=jnp.float32
    ).astype(jnp.bfloat16)
    slot_hidden = jnp.einsum(
        "rck,sc->rsk", hidden, select_down.astype(jnp.bfloat16), preferred_element_type=jnp.float32
    ).astype(jnp.bfloat16)
    weight_terms = jnp.einsum(
        "rsk,rsj->skj", tokens_slots, slot_grad, preferred_element_type=jnp.float32
    )
    weight_terms = weight_terms + jnp.einsum(
        "rsk,rsj->skj", slot_hidden, cot_slots, preferred_element_type=jnp.float32
    )
    input_terms = block_inputs(slot_grad, block_weights, block_select)
    input_sum = lax.psum_scatter(input_terms, "cols", scatter_dimension=0, tiled=True)
    input_grad = input_sum.astype(jnp.bfloat16)
    weight_sum = lax.psum_scatter(
        weight_terms.astype(jnp.bfloat16), "dp", scatter_dimension=1, tiled=True
    )
    return (input_grad, weight_sum)


def solution(mesh):
    return jax.shard_map(
        shards,
        mesh=mesh,
        in_specs=(
            P(("dp", "cols"), None),
            P(("dp", "cols"), None),
            P("cols", None, None),
            P("cols"),
            P("cols"),
            P("cols"),
        ),
        out_specs=(P(("dp", "cols"), None), P("cols", "dp", None)),
        check_vma=False,
    )
```

profile of v0, /device:TPU:0, one launch (start us, length us, event | category | flops | bytes accessed | tf_op | source)
XLA Modules:
  0.0 430.9 jit_solution(4175388226180065550)
XLA Ops:
  7.2 0.0 all-gather.5.cloned.1.call-start
  7.2 0.7 all-gather.5.cloned.1.call-update
  7.9 0.0 all-gather.3.cloned.1.call-start
  7.9 0.7 all-gather.3.cloned.1.call-update
  8.6 0.0 reduce-scatter.3.cloned.1.call-start
  9.3 0.7 compare_select_fusion
  10.0 0.7 compare_and_fusion
  10.7 0.7 and_convert_fusion.1
  11.4 0.7 and_select_fusion
  12.1 42.2 %all-gather.5.cloned.1.call-done = bf16[256,4096]{1,0:T(8,128)(2,1)} async-done(((bf16[16,4096]{1,0:T(8,128)(2,1)}), bf16[256,4096]{1,0:T(8,128)(2,1)}) %all-gather.5.cloned.1.call-update) | async-done | bytes 2097168 | tf_op jit(solution)/shard_map/all_gather | solution.py:24
  54.3 4.1 copy.25
  58.4 3.2 copy.26
  61.6 35.1 %all-gather.3.cloned.1.call-done = bf16[256,4096]{1,0:T(8,128)(2,1)} async-done(((bf16[16,4096]{1,0:T(8,128)(2,1)}), bf16[256,4096]{1,0:T(8,128)(2,1)}) %all-gather.3.cloned.1.call-update) | async-done | bytes 2097168 | tf_op jit(solution)/shard_map/all_gather | solution.py:25
  96.7 4.1 copy.22
  100.8 4.1 copy.23
  104.8 9.8 %gather_fusion.1 = bf16[256,256,128]{2,1,0:T(8,128)(2,1)} fusion(bf16[256,32,128]{2,0,1:T(8,128)(2,1)S(1)} %copy.26, s32[1024]{0:T(1024)S(1)} %pad_clamp_fusion), kind=kCustom, calls=%fused_computation.1.clone | custom fusion | bytes 33555456 | tf_op jit(solution)/shard_map/jit(_take)/gather | solution.py:36
  114.6 11.3 %gather_fusion = bf16[256,256,128]{2,1,0:T(8,128)(2,1)} fusion(bf16[256,32,128]{2,0,1:T(8,128)(2,1)} %copy.23, s32[1024]{0:T(1024)S(1)} %pad_clamp_fusion), kind=kCustom, calls=%fused_computation.clone | custom fusion | bytes 33555456 | tf_op jit(solution)/shard_map/jit(_take)/gather | solution.py:48
  125.9 19.6 %fusion.24 = bf16[256,256,128]{2,0,1:T(8,128)(2,1)} fusion(bf16[256,128,128]{2,1,0:T(8,128)(2,1)} %param.10, bf16[256,256,128]{2,1,0:T(8,128)(2,1)} %gather_fusion.1, pred[256]{0:T(512)(128)(4,1)S(1)} %compare_and_fusion), kind=kOutput, calls=%fused_computation.27 | convolution fusion | flops 2155872256 | bytes 41943296 | tf_op jit(solution)/shard_map/rsk,skj->rsj/dot_general | solution.py:39
  145.6 0.0 copy-start.2
  145.6 16.6 %fusion.21 = bf16[256,256,128]{2,0,1:T(8,128)(2,1)} fusion(bf16[256,128,128]{2,1,0:T(8,128)(2,1)} %param.10, bf16[256,256,128]{2,1,0:T(8,128)(2,1)} %gather_fusion, pred[256]{0:T(512)(128)(4,1)S(1)} %compare_and_fusion), kind=kOutput, calls=%fused_computation.26 | convolution fusion | flops 2155872256 | bytes 41943296 | tf_op jit(solution)/shard_map/rsj,skj->rsk/dot_general | solution.py:49
  162.2 0.0 copy-done.2
  162.2 17.2 %fusion.31 = f32[256,16,128]{2,1,0:T(8,128)S(1)} fusion(bf16[256,256,128]{2,0,1:T(8,128)(2,1)} %fusion.24, bf16[256]{0:T(256)(128)(2,1)S(1)} %get-tuple-element.3, s32[256]{0:T(256)S(1)} %copy-done.2), kind=kOutput, calls=%fused_computation.29 | convolution fusion | flops 268443648 | bytes 18875904 | tf_op jit(solution)/shard_map/rsj,sc->rcj/dot_general | solution.py:42
  179.5 0.0 copy-start
  179.5 1.3 copy-done
  180.8 15.0 %multiply_convert_fusion.2 = (bf16[256,8,128]{2,1,0:T(8,128)(2,1)S(1)}, bf16[256,8,128]{2,1,0:T(8,128)(2,1)S(1)}) fusion(f32[256,16,128]{2,1,0:T(8,128)S(1)} %fusion.31, bf16[256,256,128]{2,0,1:T(8,128)(2,1)} %fusion.21, bf16[256]{0:T(256)(128)(2,1)S(1)} %and_convert_fusion, s32[256]{0:T(256)S(1)} %and_select_fusion), kind=kOutput, calls=%fused_computation.36 | convolution fusion | flops 137629696 | bytes 19924480 | tf_op jit(solution)/shard_map/rsk,sc->rck/dot_general | solution.py:52
  195.8 0.0 slice-start
  195.8 0.0 slice-start.1
  195.8 8.1 %convert_bitcast_fusion.1 = bf16[256,256,128]{2,1,0:T(8,128)(2,1)} fusion(bf16[256,8,128]{2,1,0:T(8,128)(2,1)S(1)} %get-tuple-element.6, bf16[256,8,128]{2,1,0:T(8,128)(2,1)S(1)} %get-tuple-element.5, bf16[256]{0:T(256)(128)(2,1)S(1)} %get-tuple-element.3, s32[256]{0:T(256)S(1)} %copy-done.2), kind=kOutput, calls=%fused_computation.19 | convolution fusion | flops 278929408 | bytes 17827328 | tf_op jit(solution)/shard_map/rck,sc->rsk/dot_general | solution.py:58
  203.9 0.0 slice-done
  203.9 0.0 slice-done.1
  203.9 0.0 copy-start.3
  203.9 24.4 %fusion.18 = bf16[256,256,128]{2,0,1:T(8,128)(2,1)} fusion(bf16[256,128,128]{2,1,0:T(8,128)(2,1)S(1)} %bitcast.63, bf16[256,256,128]{2,1,0:T(8,128)(2,1)} %convert_bitcast_fusion.1), kind=kOutput, calls=%fused_computation.25 | convolution fusion | flops 2147483648 | bytes 41943040 | tf_op jit(solution)/shard_map/rsj,skj->rsk/dot_general | solution.py:10
  228.3 0.0 copy-done.3
  228.3 0.0 copy-start.1
  228.3 17.0 %fusion = f32[32,256,128]{2,0,1:T(8,128)S(1)} fusion(bf16[256,256,128]{2,0,1:T(8,128)(2,1)} %fusion.18, s32[256]{0:T(256)S(1)} %copy-done.3), kind=kOutput, calls=%fused_computation.2 | convolution fusion | flops 536879104 | bytes 20972544 | tf_op jit(solution)/shard_map/rsk,sb->rbk/dot_general | solution.py:13
  245.3 5.8 %copy.58 = f32[32,8,32,128]{3,1,2,0:T(8,128)} copy(f32[32,8,32,128]{3,2,1,0:T(8,128)S(1)} %bitcast.61) | data formatting | bytes 8388608
  251.1 0.0 reduce-scatter.3.cloned.1.call-update
  251.2 0.0 reduce-scatter.5.cloned.1.call-start
  251.2 0.0 copy-done.1
  251.2 8.7 %convert_bitcast_fusion = bf16[256,256,128]{2,1,0:T(8,128)(2,1)} fusion(f32[256,16,128]{2,1,0:T(8,128)S(1)} %copy-done.1, bf16[256]{0:T(256)(128)(2,1)S(1)} %and_convert_fusion, s32[256]{0:T(256)S(1)} %and_select_fusion), kind=kOutput, calls=%fused_computation.18 | convolution fusion | flops 144183296 | bytes 18875904 | tf_op jit(solution)/shard_map/rck,sc->rsk/dot_general | solution.py:61
  259.9 29.4 %fusion.6 = f32[256,128,128]{2,1,0:T(8,128)} fusion(bf16[256,256,128]{2,1,0:T(8,128)(2,1)} %convert_bitcast_fusion.1, bf16[256,256,128]{2,1,0:T(8,128)(2,1)} %gather_fusion.1, pred[256]{0:T(512)(128)(4,1)S(1)} %compare_and_fusion), kind=kOutput, calls=%fused_computation.8 | convolution fusion | flops 2155872256 | bytes 50331904 | tf_op jit(solution)/shard_map/rsk,rsj->skj/dot_general | solution.py:64
  289.3 27.1 %add_convert_fusion = bf16[256,128,128]{2,1,0:T(8,128)(2,1)} fusion(f32[256,128,128]{2,1,0:T(8,128)} %fusion.6, bf16[256,256,128]{2,1,0:T(8,128)(2,1)} %convert_bitcast_fusion, bf16[256,256,128]{2,1,0:T(8,128)(2,1)} %gather_fusion, pred[256]{0:T(512)(128)(4,1)S(1)} %compare_and_fusion), kind=kOutput, calls=%fused_computation.17 | convolution fusion | flops 2164260864 | bytes 58720512 | tf_op jit(solution)/shard_map/rsk,rsj->skj/dot_general | solution.py:67
  316.4 0.0 reduce-scatter.5.cloned.1.call-update
  316.4 6.4 %reduce-scatter.3.cloned.1.call-done = f32[16,4096]{1,0:T(8,128)} async-done(((f32[256,4096]{1,0:T(8,128)}), f32[16,4096]{1,0:T(8,128)}) %reduce-scatter.3.cloned.1.call-update) | async-done | bytes 262160 | tf_op jit(solution)/shard_map/reduce_scatter | solution.py:71
  322.8 1.6 convert_element_type.54
  324.4 99.5 %reduce-scatter.5.cloned.1.call-done = bf16[256,64,128]{2,1,0:T(8,128)(2,1)} async-done(((bf16[256,128,128]{2,1,0:T(8,128)(2,1)}), bf16[256,64,128]{2,1,0:T(8,128)(2,1)}) %reduce-scatter.5.cloned.1.call-update) | async-done | bytes 4194320 | tf_op jit(solution)/shard_map/reduce_scatter | solution.py:73
  (3 shorter events, 0.0 us)
Async XLA Ops:
  7.2 47.2 %all-gather.5.cloned.1.call-start = ((), (), s32[]{:S(2)}) async-start(), calls=%async_computation.3 | async-start | bytes 2228224 | tf_op jit(solution)/shard_map/all_gather | solution.py:24
  7.9 88.8 %all-gather.3.cloned.1.call-start = ((), (), s32[]{:S(2)}) async-start(), calls=%async_computation.2 | async-start | bytes 2228224 | tf_op jit(solution)/shard_map/all_gather | solution.py:25
  8.6 314.2 %reduce-scatter.3.cloned.1.call-start = ((), (), s32[]{:S(2)}) async-start(), calls=%async_computation.4 | async-start | bytes 4456448 | tf_op jit(solution)/shard_map/reduce_scatter | solution.py:71
  145.6 16.6 %copy-start.2 = (s32[256]{0:T(256)S(1)}, s32[256]{0:T(256)}, u32[]{:S(2)}) copy-start(s32[256]{0:T(256)} %param.12) | copy-start | bytes 3076
  179.5 1.3 copy-start
  195.8 8.1 %slice-start = ((s8[8388608]{0:T(1024)(128)(4,1)}), s8[4194304]{0:T(1024)(128)(4,1)S(1)}, s32[]{:S(2)}) async-start(s8[8388608]{0:T(1024)(128)(4,1)} %bitcast.62), calls=%async_computation.6 | async-start | bytes 8388608
  195.8 8.1 %slice-start.1 = ((s8[8388608]{0:T(1024)(128)(4,1)}), s8[4194304]{0:T(1024)(128)(4,1)S(1)}, s32[]{:S(2)}) async-start(s8[8388608]{0:T(1024)(128)(4,1)} %bitcast.62), calls=%async_computation.7 | async-start | bytes 8388608
  203.9 24.4 %copy-start.3 = (s32[256]{0:T(256)S(1)}, s32[256]{0:T(256)}, u32[]{:S(2)}) copy-start(s32[256]{0:T(256)} %param.11) | copy-start | bytes 3076
  228.3 22.9 %copy-start.1 = (f32[256,16,128]{2,1,0:T(8,128)S(1)}, f32[256,16,128]{2,1,0:T(8,128)}, u32[]{:S(2)}) copy-start(f32[256,16,128]{2,1,0:T(8,128)} %copy-done) | copy-start | bytes 6291460
  251.2 172.8 %reduce-scatter.5.cloned.1.call-start = ((), (), s32[]{:S(2)}) async-start(), calls=%async_computation.5 | async-start | bytes 12582912 | tf_op jit(solution)/shard_map/reduce_scatter | solution.py:73
Sparse Core Ops, SparseCore 0:
  10.1 44.1 all-gather.4
  56.5 40.1 all-gather.2
  251.3 71.4 reduce-scatter.2
  325.5 98.3 reduce-scatter.4
where the time goes:
time: 438 us; the launch traced here: 431 us
  waiting for transfers between devices  185 us (42%)
  matrix products  183 us (42%)
  local copies, waits for them, and re-layouts  43.6 us (10%)
  between operations  14.9 us (3%)
  other arithmetic  4.38 us (1%)
    reduce_scatter x1, waiting for transfers between devices, shards(): lax.psum_scatter(weight_terms.astype(jnp.bfloat16), 'dp', scatter_dimensi...  99.5 us
    all_gather x1, waiting for transfers between devices, shards(): lax.all_gather(tokens, 'cols', axis=0, tiled=True)  42.2 us
    all_gather x1, waiting for transfers between devices, shards(): lax.all_gather(cotangent, 'cols', axis=0, tiled=True)  35.1 us
    dot_general x1, matrix products, shards(): jnp.einsum('rsk,rsj->skj', tokens_slots, slot_grad, preferred_element_typ...  29.4 us
    dot_general x1, matrix products, shards(): jnp.einsum('rsk,rsj->skj', slot_hidden, cot_slots, preferred_element_type...  27.1 us
    dot_general x1, matrix products, block_inputs(): jnp.einsum('rsj,skj->rsk', grad_rows, weights, preferred_element_type=jnp...  24.4 us
    dot_general x1, matrix products, shards(): jnp.einsum('rsk,skj->rsj', tokens_slots, block_weights, preferred_element...  19.6 us
    dot_general x1, matrix products, shards(): gate_up = jnp.einsum('rsj,sc->rcj', products, select_up)  17.2 us
  transfers between devices with their start and end apart: 4, of which 4 were waited for; matrix products, arithmetic and copies ran while one was open for 18% of the time, Pallas kernels for 0%

commit v1 on v0

--- a/solution.py
+++ b/solution.py
@@ -1,6 +1,10 @@
+import functools
+
 import jax
 import jax.numpy as jnp
 from jax import lax
+from jax.experimental import pallas as pl
+from jax.experimental.pallas import tpu as pltpu
 from jax.sharding import PartitionSpec as P
 
 SPC = 32
@@ -76,9 +80,388 @@
     return (input_grad, weight_sum)
 
 
+MESH = pl.DeviceIdType.MESH
+F32 = jnp.float32
+BF16 = jnp.bfloat16
+NT = (((1,), (1,)), ((), ()))
+
+
+def layer_kernel(
+    n_cols, table_ref, slots_ref, tok_ref, cot_ref, w_ref, in_ref, wg_ref,
+    tok, cot, blocks, wgu, wd, grads, hid, acc, sib_out, sib_in, chip_sum, a2a,
+    fin_out, fin_in, lhs, hid_t,
+    w_sem, own_sem, ring_send, ring_recv, sib_send, sib_recv,
+    x_send, x_recv, half_send, half_recv, a2a_send, a2a_recv, fin_send, fin_recv,
+):
+    chips = n_cols // 2
+    steps = chips // 2
+    rows = tok_ref.shape[0]
+    group_rows = rows * n_cols
+    features = tok_ref.shape[1]
+    width = blocks.shape[2]
+    part = blocks.shape[1]
+    n_f = features // width
+    hidden = wd.shape[0]
+    n_h = hidden // width
+    zero_at = blocks.shape[0] - 1
+    half = features // 2
+    dp = lax.axis_index("dp")
+    col = lax.axis_index("cols")
+    core = col % 2
+    chip = col // 2
+    place = jnp.where(chip % 2 == 0, chip // 2, chips - 1 - chip // 2)
+
+    def chip_at(p):
+        p = (p + 2 * chips) % chips
+        return jnp.where(p < steps, 2 * p, 2 * (chips - 1 - p) + 1)
+
+    right = chip_at(place + 1) * 2 + core
+    left = chip_at(place - 1) * 2 + core
+    sibling = chip * 2 + 1 - core
+    sides = ((tok_ref, tok), (cot_ref, cot))
+
+    barrier = pltpu.get_barrier_semaphore()
+    for r in range(1, chips):
+        pl.semaphore_signal(barrier, inc=1, device_id=(dp, ((chip + r) % chips) * 2 + core), device_id_type=MESH)
+    pl.semaphore_signal(barrier, inc=1, device_id=(dp, sibling), device_id_type=MESH)
+    pl.semaphore_signal(barrier, inc=1, device_id=(1 - dp, col), device_id_type=MESH)
+    pl.semaphore_wait(barrier, chips + 1)
+
+    w_copy = pltpu.make_async_copy(w_ref, blocks.at[pl.ds(0, w_ref.shape[0])], w_sem)
+    w_copy.start()
+
+    def ring(g, direction, s, a):
+        origin = chip_at(place - s if direction == 0 else place + s) * 2 + core
+        block = sides[a][1].at[g, origin]
+        return pltpu.make_async_remote_copy(
+            src_ref=block, dst_ref=block,
+            send_sem=ring_send.at[g, direction, s, a], recv_sem=ring_recv.at[g, direction, s, a],
+            device_id=(dp, right if direction == 0 else left), device_id_type=MESH,
+        )
+
+    def ring_arrival(g, direction, s, a):
+        origin = chip_at(place - 1 - s if direction == 0 else place + 1 + s) * 2 + core
+        block = sides[a][1].at[g, origin]
+        return pltpu.make_async_remote_copy(
+            src_ref=block, dst_ref=block,
+            send_sem=ring_send.at[g, direction, s, a], recv_sem=ring_recv.at[g, direction, s, a],
+            device_id=(dp, right if direction == 0 else left), device_id_type=MESH,
+        )
+
+    def share(g, k, a, lane):
+        origin = chip_at(place - k) * 2 + lane
+        block = sides[a][1].at[g, origin]
+        return pltpu.make_async_remote_copy(
+            src_ref=block, dst_ref=block,
+            send_sem=sib_send.at[g, k, a], recv_sem=sib_recv.at[g, k, a],
+            device_id=(dp, sibling), device_id_type=MESH,
+        )
+
+    def cross(a):
+        return pltpu.make_async_remote_copy(
+            src_ref=sides[a][1].at[0, col], dst_ref=sides[a][1].at[1, col],
+            send_sem=x_send.at[a], recv_sem=x_recv.at[a],
+            device_id=(1 - dp, col), device_id_type=MESH,
+        )
+
+    def first(g):
+        for a in range(2):
+            for direction in range(2):
+                ring(g, direction, 0, a).start()
+        for a in range(2):
+            share(g, 0, a, core).start()
+
+    def pass_on(g, s, direction, a):
+        ring_arrival(g, direction, s, a).wait_recv()
+
+        far = steps - 1 if a == direction else steps - 2
+
+        @pl.when(s < far)
+        def _():
+            ring(g, direction, s + 1, a).start()
+
+        k = 1 + s if direction == 0 else chips - 1 - s
+        share(g, k, a, core).start()
+
+    def advance(g, s):
+        pass_on(g, s, 0, 0)
+        pass_on(g, s, 1, 1)
+
+        @pl.when(s < steps - 1)
+        def _():
+            pass_on(g, s, 0, 1)
+            pass_on(g, s, 1, 0)
+
+    def all_shared(g):
+        for a in range(2):
+            @pl.loop(0, chips)
+            def _(k):
+                share(g, k, a, 1 - core).wait_recv()
+
+    for a in range(2):
+        own = pltpu.make_async_copy(sides[a][0], sides[a][1].at[0, col], own_sem.at[a])
+        own.start()
+        own.wait()
+    first(0)
+    cross(0).start()
+    cross(1).start()
+    blocks[zero_at] = jnp.zeros((part, width), BF16)
+    w_copy.wait()
+
+    pieces = width // part
+
+    def spread(h, f):
+        at = pl.multiple_of(f * width, width)
+        hid_at = pl.multiple_of(h * width, width)
+        for k in range(3):
+            index = table_ref[(k * n_h + h) * n_f + f]
+            for piece in range(pieces):
+                value = blocks[jnp.minimum(index * pieces + piece, zero_at)]
+                if k < 2:
+                    wgu[pl.ds(pl.multiple_of(at + piece * part, part), part),
+                        pl.ds(pl.multiple_of(k * hidden + hid_at, width), width)] = value
+                else:
+                    wd[pl.ds(pl.multiple_of(hid_at + piece * part, part), part), pl.ds(at, width)] = value
+
+    per_step = n_h // steps
+
+    @pl.loop(0, steps)
+    def _(s):
+        @pl.loop(0, n_f)
+        def _(f):
+            for j in range(per_step):
+                spread(s * per_step + j, f)
+
+        advance(0, s)
+
+    all_shared(0)
+    for a in range(2):
+        cross(a).wait_recv()
+    first(1)
+
+    span = hidden // steps
+
+    def forward(g, n):
+        at = pl.multiple_of(n * span, span)
+        x = tok[g].reshape(group_rows, features)
+        gate = jnp.dot(x, wgu[:, pl.ds(at, span)], preferred_element_type=F32)
+        up = jnp.dot(x, wgu[:, pl.ds(pl.multiple_of(hidden + at, span), span)], preferred_element_type=F32)
+        back = lax.dot_general(
+            cot[g].reshape(group_rows, features), wd[pl.ds(at, span), :], NT, preferred_element_type=F32
+        )
+        sig = jax.nn.sigmoid(gate)
+        silu = gate * sig
+        hid[g, :, pl.ds(at, span)] = (silu * up).astype(BF16)
+        grads[g, :, pl.ds(at, span)] = (back * up * sig * (1.0 + gate * (1.0 - sig))).astype(BF16)
+        grads[g, :, pl.ds(pl.multiple_of(hidden + at, span), span)] = (back * silu).astype(BF16)
+
+    @pl.loop(0, steps)
+    def _(s):
+        forward(0, s)
+        advance(1, s)
+
+    chunk = half // 4
+
+    def terms(at):
+        return lax.dot_general(grads[0], wgu[pl.ds(at, chunk), :], NT, preferred_element_type=F32)
+
+    @pl.loop(0, 4)
+    def _(i):
+        at = pl.multiple_of(i * chunk, chunk)
+        src = pl.multiple_of((1 - core) * half + at, chunk)
+        sib_out[:, pl.ds(at, chunk)] = terms(src).astype(BF16)
+
+    to_sibling = pltpu.make_async_remote_copy(
+        src_ref=sib_out, dst_ref=sib_in, send_sem=half_send, recv_sem=half_recv,
+        device_id=(dp, sibling), device_id_type=MESH,
+    )
+    to_sibling.start()
+
+    @pl.loop(0, 4)
+    def _(i):
+        at = pl.multiple_of(i * chunk, chunk)
+        acc[:, pl.ds(at, chunk)] = terms(pl.multiple_of(core * half + at, chunk))
+
+    to_sibling.wait_recv()
+    chip_rows = group_rows // chips
+
+    @pl.loop(0, chips)
+    def _(c):
+        at = pl.ds(pl.multiple_of(c * chip_rows, chip_rows), chip_rows)
+        total = acc[at, :] + sib_in[at, :].astype(F32)
+        acc[at, :] = total
+        chip_sum[c] = total.astype(BF16)
+
+    def spread_sum(r):
+        other = (chip + r) % chips
+        return pltpu.make_async_remote_copy(
+            src_ref=chip_sum.at[other], dst_ref=a2a.at[r],
+            send_sem=a2a_send.at[r], recv_sem=a2a_recv.at[r],
+            device_id=(dp, other * 2 + core), device_id_type=MESH,
+        )
+
+    @pl.loop(1, chips)
+    def _(r):
+        spread_sum(r).start()
+
+    all_shared(1)
+
+    @pl.loop(0, steps)
+    def _(s):
+        forward(1, s)
+
+    def take_part(block):
+        out = block[:part]
+        for i in range(1, width // part):
+            out = jnp.where(dp == i, block[i * part:(i + 1) * part], out)
+        return out
+
+    for g in range(2):
+        for h in range(n_h):
+            hid_t[pl.ds(h * part, part), pl.ds(g * group_rows, group_rows)] = take_part(
+                hid[g, :, pl.ds(h * width, width)].T
+            )
+    four = 4
+
+    @pl.loop(0, n_f // four)
+    def _(i):
+        at = pl.multiple_of(i * four * width, four * width)
+        for g in range(2):
+            for b in range(four):
+                piece = tok[g, :, :, pl.ds(pl.multiple_of(at + b * width, width), width)]
+                lhs[pl.ds(b * part, part), pl.ds(g * group_rows, group_rows)] = take_part(
+                    piece.reshape(group_rows, width).T
+                )
+        for n in range(2 * n_h // 4):
+            cut = slice(n * 4 * width, (n + 1) * 4 * width)
+            out = jnp.dot(
+                lhs[...], grads[:, :, cut].reshape(2 * group_rows, 4 * width), preferred_element_type=F32
+            ).astype(BF16)
+            for h in range(4):
+                for b in range(four):
+                    blocks[(n * 4 + h) * n_f + i * four + b] = out[
+                        b * part:(b + 1) * part, h * width:(h + 1) * width
+                    ]
+        c = cot[:, :, :, pl.ds(at, four * width)].reshape(2 * group_rows, four * width)
+        out = jnp.dot(hid_t[...], c, preferred_element_type=F32).astype(BF16)
+        for h in range(n_h):
+            for b in range(four):
+                blocks[(2 * n_h + h) * n_f + i * four + b] = out[
+                    h * part:(h + 1) * part, b * width:(b + 1) * width
+                ]
+
+    @pl.loop(0, wg_ref.shape[0], unroll=8)
+    def _(s):
+        wg_ref[s] = blocks[slots_ref[s]]
+
+    @pl.loop(1, chips)
+    def _(r):
+        spread_sum(r).wait_recv()
+
+    total = acc[pl.ds(pl.multiple_of(chip * chip_rows, chip_rows), chip_rows), :]
+    for r in range(1, chips):
+        total = total + a2a[r].astype(F32)
+    total = total.astype(BF16)
+    low, high = total[:rows], total[rows:]
+    fin_out[...] = jnp.where(core == 0, high, low)
+    fin = pltpu.make_async_remote_copy(
+        src_ref=fin_out, dst_ref=fin_in, send_sem=fin_send, recv_sem=fin_recv,
+        device_id=(dp, sibling), device_id_type=MESH,
+    )
+    fin.start()
+    in_ref[:, pl.ds(pl.multiple_of(core * half, half), half)] = jnp.where(core == 0, low, high)
+    fin.wait()
+    in_ref[:, pl.ds(pl.multiple_of((1 - core) * half, half), half)] = fin_in[...]
+
+    to_sibling.wait_send()
+
+    @pl.loop(1, chips)
+    def _(r):
+        spread_sum(r).wait_send()
+
+    for a in range(2):
+        cross(a).wait_send()
+    for g in range(2):
+        for a in range(2):
+            for direction in range(2):
+                @pl.loop(0, steps if a == direction else steps - 1)
+                def _(s):
+                    ring(g, direction, s, a).wait_send()
+
+            @pl.loop(0, chips)
+            def _(k):
+                share(g, k, a, core).wait_send()
+
+
+def kernel_shards(n_cols, tokens, cotangent, block_weights, slot_block, slot_target, counts):
+    n_slots, width = block_weights.shape[:2]
+    n_dp = 2
+    part = width // n_dp
+    rows, features = tokens.shape
+    n_f = features // width
+    hidden_blocks = n_slots // SPC
+    hidden = hidden_blocks * width
+    places = 3 * hidden_blocks * n_f
+    place = slot_target * n_f + slot_block
+    number = jnp.arange(n_slots, dtype=jnp.int32)
+    live = number < counts[0]
+    hit = (place[None, :] == jnp.arange(places, dtype=jnp.int32)[:, None]) & live[None, :]
+    table = places + jnp.sum(jnp.where(hit, number[None, :] - places, 0), axis=1)
+    slots = jnp.where(live, place, places)
+    chips = n_cols // 2
+    group_rows = rows * n_cols
+    half = features // 2
+    dma = pltpu.SemaphoreType.DMA
+    vmem = pl.BlockSpec(memory_space=pltpu.VMEM)
+    smem = pl.BlockSpec(memory_space=pltpu.SMEM)
+    return pl.pallas_call(
+        functools.partial(layer_kernel, n_cols),
+        out_shape=(
+            jax.ShapeDtypeStruct((rows, features), BF16),
+            jax.ShapeDtypeStruct((n_slots, part, width), BF16),
+        ),
+        in_specs=[smem, smem, vmem, vmem, pl.BlockSpec(memory_space=pl.ANY)],
+        out_specs=(vmem, vmem),
+        scratch_shapes=[
+            pltpu.VMEM((n_dp, n_cols, rows, features), BF16),
+            pltpu.VMEM((n_dp, n_cols, rows, features), BF16),
+            pltpu.VMEM((places + 1, part, width), BF16),
+            pltpu.VMEM((features, 2 * hidden), BF16),
+            pltpu.VMEM((hidden, features), BF16),
+            pltpu.VMEM((n_dp, group_rows, 2 * hidden), BF16),
+            pltpu.VMEM((n_dp, group_rows, hidden), BF16),
+            pltpu.VMEM((group_rows, half), F32),
+            pltpu.VMEM((group_rows, half), BF16),
+            pltpu.VMEM((group_rows, half), BF16),
+            pltpu.VMEM((chips, group_rows // chips, half), BF16),
+            pltpu.VMEM((chips, group_rows // chips, half), BF16),
+            pltpu.VMEM((rows, half), BF16),
+            pltpu.VMEM((rows, half), BF16),
+            pltpu.VMEM((4 * part, n_dp * group_rows), BF16),
+            pltpu.VMEM((hidden // n_dp, n_dp * group_rows), BF16),
+            dma, dma((2,)),
+            dma((2, 2, chips // 2, 2)), dma((2, 2, chips // 2, 2)),
+            dma((2, chips, 2)), dma((2, chips, 2)),
+            dma((2,)), dma((2,)), dma, dma, dma((chips,)), dma((chips,)), dma, dma,
+        ],
+        compiler_params=pltpu.CompilerParams(
+            collective_id=0, has_side_effects=True, vmem_limit_bytes=67043328
+        ),
+    )(table, slots, tokens, cotangent, block_weights.reshape(n_slots * n_dp, part, width))
+
+
 def solution(mesh):
+    n_dp, n_cols = mesh.shape["dp"], mesh.shape["cols"]
+    paired = n_dp == 2 and n_cols % 4 == 0
+
+    def body(*args):
+        tokens, weights = args[0], args[2]
+        if paired and tokens.shape[0] % 16 == 0 and weights.shape[0] // SPC % (n_cols // 4) == 0:
+            return kernel_shards(n_cols, *args)
+        return shards(*args)
+
     return jax.shard_map(
-        shards,
+        body,
         mesh=mesh,
         in_specs=(
             P(("dp", "cols"), None),

time: 438 us -> 97.6 us (0.22)
  the two profiles are of different devices: /device:TPU:0 before, /device:TPU:13 now
where the time goes in v1:
time: 97.6 us; the launch traced here: 97.3 us
  Pallas kernels  87.2 us (89%)
  local copies, waits for them, and re-layouts  6.73 us (7%)
  other arithmetic  2.1 us (2%)
  between operations  1.3 us (1%)
    pallas_call x1, Pallas kernels, kernel_shards(): pl.pallas_call(functools.partial(layer_kernel, n_cols), out_shape=(jax.Sh...  87.2 us
    unnamed x2, local copies, waits for them, and re-layouts  6.73 us

profile of v1, /device:TPU:13, one launch (start us, length us, event | category | flops | bytes accessed | tf_op | source)
XLA Modules:
  0.0 97.3 jit_solution(16016410512100032346)
XLA Ops:
  1.3 1.3 %broadcast_select_fusion = (s32[256]{0:T(256)}, s32[256]{0:T(256)S(1)}, s32[256]{0:T(256)S(1)}) fusion(s32[]{:T(128)} %bitcast.3, s32[256]{0:T(256)} %param.9, s32[256]{0:T(256)} %param.10), kind=kLoop, calls=%fused_computation.7 | loop fusion | flops 1280 | bytes 5124 | tf_op jit(solution)/shard_map/jit(_where)/select_n | solution.py:410
  2.6 0.2 select_reduce_fusion
  2.8 0.6 broadcast_add_fusion.table_ref
  3.4 87.2 %shard_map.77 = (bf16[16,4096]{1,0:T(8,128)(2,1)}, bf16[256,64,128]{2,1,0:T(8,128)(2,1)}) custom-call(s32[768]{0:T(1024)} %broadcast_add_fusion.table_ref, s32[256]{0:T(256)} %get-tuple-element.2.slots_ref, bf16[16,4096]{1,0:T(8,128)(2,1)} %tok_ref.1, bf16[16,4096]{1,0:T(8,128)(2,1)} %cot_ref.1, bf16[512,64,128]{2,1,0:T(8,128)(2,1)} %bitcast.4), custom_call_target="tpu_custom_call" | custom-call | tf_op jit(solution)/shard_map/pallas_call | solution.py:417
  90.6 1.6 %copy.11 = bf16[16,4096]{1,0:T(8,128)(2,1)} copy(bf16[16,4096]{1,0:T(8,128)(2,1)} %get-tuple-element.7) | data formatting | bytes 262144
  92.2 5.2 %copy.12 = bf16[256,64,128]{2,1,0:T(8,128)(2,1)} copy(bf16[256,64,128]{2,1,0:T(8,128)(2,1)} %get-tuple-element.8) | data formatting | bytes 8388608
  (1 shorter events, 0.0 us)

commit v2 on v1

--- a/solution.py
+++ b/solution.py
@@ -84,11 +84,12 @@
 F32 = jnp.float32
 BF16 = jnp.bfloat16
 NT = (((1,), (1,)), ((), ()))
+CHUNKS = 4
 
 
 def layer_kernel(
     n_cols, table_ref, slots_ref, tok_ref, cot_ref, w_ref, in_ref, wg_ref,
-    tok, cot, blocks, wgu, wd, grads, hid, acc, sib_out, sib_in, chip_sum, a2a,
+    tok, cot, blocks, wgu, wd, grads, hid, pre, acc, sib_out, sib_in, chip_sum, a2a,
     fin_out, fin_in, lhs, hid_t,
     w_sem, own_sem, ring_send, ring_recv, sib_send, sib_recv,
     x_send, x_recv, half_send, half_recv, a2a_send, a2a_recv, fin_send, fin_recv,
@@ -130,81 +131,94 @@
     w_copy = pltpu.make_async_copy(w_ref, blocks.at[pl.ds(0, w_ref.shape[0])], w_sem)
     w_copy.start()
 
-    def ring(g, direction, s, a):
-        origin = chip_at(place - s if direction == 0 else place + s) * 2 + core
-        block = sides[a][1].at[g, origin]
+    def piece(g, origin, a):
+        at = pl.ds((a % 2) * half, half)
+        return sides[a // 2][1].at[g, origin * 2 + core, :, at]
+
+    def ring_copy(g, origin, direction, s, a):
+        block = piece(g, origin, a)
         return pltpu.make_async_remote_copy(
             src_ref=block, dst_ref=block,
             send_sem=ring_send.at[g, direction, s, a], recv_sem=ring_recv.at[g, direction, s, a],
             device_id=(dp, right if direction == 0 else left), device_id_type=MESH,
         )
 
+    def ring(g, direction, s, a):
+        return ring_copy(g, chip_at(place - s if direction == 0 else place + s), direction, s, a)
+
     def ring_arrival(g, direction, s, a):
-        origin = chip_at(place - 1 - s if direction == 0 else place + 1 + s) * 2 + core
-        block = sides[a][1].at[g, origin]
-        return pltpu.make_async_remote_copy(
-            src_ref=block, dst_ref=block,
-            send_sem=ring_send.at[g, direction, s, a], recv_sem=ring_recv.at[g, direction, s, a],
-            device_id=(dp, right if direction == 0 else left), device_id_type=MESH,
-        )
-
-    def share(g, k, a, lane):
-        origin = chip_at(place - k) * 2 + lane
-        block = sides[a][1].at[g, origin]
+        return ring_copy(g, chip_at(place - 1 - s if direction == 0 else place + 1 + s), direction, s, a)
+
+    def share_copy(g, k, a, lane):
+        at = pl.ds((a % 2) * half, half)
+        block = sides[a // 2][1].at[g, chip_at(place - k) * 2 + lane, :, at]
         return pltpu.make_async_remote_copy(
             src_ref=block, dst_ref=block,
             send_sem=sib_send.at[g, k, a], recv_sem=sib_recv.at[g, k, a],
             device_id=(dp, sibling), device_id_type=MESH,
         )
 
-    def cross(a):
+    def share(g, k, a):
+        return share_copy(g, k, a, core)
+
+    def cross(k, a):
+        origin = chip_at(place - k)
         return pltpu.make_async_remote_copy(
-            src_ref=sides[a][1].at[0, col], dst_ref=sides[a][1].at[1, col],
-            send_sem=x_send.at[a], recv_sem=x_recv.at[a],
+            src_ref=piece(0, origin, a), dst_ref=piece(1, origin, a),
+            send_sem=x_send.at[k, a], recv_sem=x_recv.at[k, a],
             device_id=(1 - dp, col), device_id_type=MESH,
         )
 
-    def first(g):
-        for a in range(2):
+    def first(g, arr):
+        for a in (2 * arr, 2 * arr + 1):
             for direction in range(2):
                 ring(g, direction, 0, a).start()
-        for a in range(2):
-            share(g, 0, a, core).start()
-
-    def pass_on(g, s, direction, a):
-        ring_arrival(g, direction, s, a).wait_recv()
-
-        far = steps - 1 if a == direction else steps - 2
+        for a in (2 * arr, 2 * arr + 1):
+            share(g, 0, a).start()
+            if g == 0:
+                cross(0, a).start()
+
+    def pass_on(s, direction, a):
+        ring_arrival(0, direction, s, a).wait_recv()
+
+        far = steps - 1 if a % 2 == direction else steps - 2
 
         @pl.when(s < far)
         def _():
-            ring(g, direction, s + 1, a).start()
+            ring(0, direction, s + 1, a).start()
 
         k = 1 + s if direction == 0 else chips - 1 - s
-        share(g, k, a, core).start()
-
-    def advance(g, s):
-        pass_on(g, s, 0, 0)
-        pass_on(g, s, 1, 1)
+        share(0, k, a).start()
+
+        @pl.when(s > 0)
+        def _():
+            cross(k, a).start()
+
+    def advance(s, arr):
+        for direction in range(2):
+            pass_on(s, direction, 2 * arr + direction)
 
         @pl.when(s < steps - 1)
         def _():
-            pass_on(g, s, 0, 1)
-            pass_on(g, s, 1, 0)
-
-    def all_shared(g):
-        for a in range(2):
-            @pl.loop(0, chips)
-            def _(k):
-                share(g, k, a, 1 - core).wait_recv()
+            for direction in range(2):
+                pass_on(s, direction, 2 * arr + 1 - direction)
+
+    def all_shared(g, arr):
+        @pl.loop(0, chips)
+        def _(k):
+            for a in (2 * arr, 2 * arr + 1):
+                share_copy(g, k, a, 1 - core).wait_recv()
+
+    def crossed(k):
+        for a in range(4):
+            cross(k, a).wait_recv()
+            share(1, k, a).start()
 
     for a in range(2):
         own = pltpu.make_async_copy(sides[a][0], sides[a][1].at[0, col], own_sem.at[a])
         own.start()
         own.wait()
-    first(0)
-    cross(0).start()
-    cross(1).start()
+    first(0, 0)
     blocks[zero_at] = jnp.zeros((part, width), BF16)
     w_copy.wait()
 
@@ -232,20 +246,24 @@
             for j in range(per_step):
                 spread(s * per_step + j, f)
 
-        advance(0, s)
-
-    all_shared(0)
-    for a in range(2):
-        cross(a).wait_recv()
-    first(1)
-
+        advance(s, 0)
+
+        @pl.when(s == steps // 2 - 1)
+        def _():
+            first(0, 1)
+
+    all_shared(0, 0)
     span = hidden // steps
 
-    def forward(g, n):
+    def before(g, n):
         at = pl.multiple_of(n * span, span)
         x = tok[g].reshape(group_rows, features)
         gate = jnp.dot(x, wgu[:, pl.ds(at, span)], preferred_element_type=F32)
         up = jnp.dot(x, wgu[:, pl.ds(pl.multiple_of(hidden + at, span), span)], preferred_element_type=F32)
+        return gate, up
+
+    def after(g, n, gate, up):
+        at = pl.multiple_of(n * span, span)
         back = lax.dot_general(
             cot[g].reshape(group_rows, features), wd[pl.ds(at, span), :], NT, preferred_element_type=F32
         )
@@ -257,58 +275,87 @@
 
     @pl.loop(0, steps)
     def _(s):
-        forward(0, s)
-        advance(1, s)
-
-    chunk = half // 4
+        gate, up = before(0, s)
+        pre[s, 0] = gate
+        pre[s, 1] = up
+        advance(s, 1)
+
+    for a in range(4):
+        cross(0, a).wait_recv()
+    first(1, 0)
+    first(1, 1)
+    all_shared(0, 1)
+
+    @pl.loop(0, steps)
+    def _(s):
+        after(0, s, pre[s, 0], pre[s, 1])
+
+    crossed(2)
+    crossed(chips - 2)
+
+    chunk = half // CHUNKS
+    chip_rows = group_rows // chips
 
     def terms(at):
         return lax.dot_general(grads[0], wgu[pl.ds(at, chunk), :], NT, preferred_element_type=F32)
 
-    @pl.loop(0, 4)
+    def to_sibling(i):
+        return pltpu.make_async_remote_copy(
+            src_ref=sib_out.at[i], dst_ref=sib_in.at[i], send_sem=half_send.at[i], recv_sem=half_recv.at[i],
+            device_id=(dp, sibling), device_id_type=MESH,
+        )
+
+    def spread_sum(r, i):
+        other = (chip + r) % chips
+        return pltpu.make_async_remote_copy(
+            src_ref=chip_sum.at[i, other], dst_ref=a2a.at[i, r],
+            send_sem=a2a_send.at[i, r], recv_sem=a2a_recv.at[i, r],
+            device_id=(dp, other * 2 + core), device_id_type=MESH,
+        )
+
+    def pair_sum(i):
+        to_sibling(i).wait_recv()
+
+        @pl.loop(0, chips)
+        def _(c):
+            at = pl.ds(pl.multiple_of(c * chip_rows, chip_rows), chip_rows)
+            total = acc[i, at, :] + sib_in[i, at, :].astype(F32)
+            acc[i, at, :] = total
+            chip_sum[i, c] = total.astype(BF16)
+
+        @pl.loop(1, chips)
+        def _(r):
+            spread_sum(r, i).start()
+
+    @pl.loop(0, CHUNKS)
     def _(i):
         at = pl.multiple_of(i * chunk, chunk)
-        src = pl.multiple_of((1 - core) * half + at, chunk)
-        sib_out[:, pl.ds(at, chunk)] = terms(src).astype(BF16)
-
-    to_sibling = pltpu.make_async_remote_copy(
-        src_ref=sib_out, dst_ref=sib_in, send_sem=half_send, recv_sem=half_recv,
-        device_id=(dp, sibling), device_id_type=MESH,
-    )
-    to_sibling.start()
-
-    @pl.loop(0, 4)
-    def _(i):
-        at = pl.multiple_of(i * chunk, chunk)
-        acc[:, pl.ds(at, chunk)] = terms(pl.multiple_of(core * half + at, chunk))
-
-    to_sibling.wait_recv()
-    chip_rows = group_rows // chips
-
-    @pl.loop(0, chips)
-    def _(c):
-        at = pl.ds(pl.multiple_of(c * chip_rows, chip_rows), chip_rows)
-        total = acc[at, :] + sib_in[at, :].astype(F32)
-        acc[at, :] = total
-        chip_sum[c] = total.astype(BF16)
-
-    def spread_sum(r):
-        other = (chip + r) % chips
-        return pltpu.make_async_remote_copy(
-            src_ref=chip_sum.at[other], dst_ref=a2a.at[r],
-            send_sem=a2a_send.at[r], recv_sem=a2a_recv.at[r],
-            device_id=(dp, other * 2 + core), device_id_type=MESH,
-        )
-
-    @pl.loop(1, chips)
-    def _(r):
-        spread_sum(r).start()
-
-    all_shared(1)
+        sib_out[i] = terms(pl.multiple_of((1 - core) * half + at, chunk)).astype(BF16)
+        to_sibling(i).start()
+        acc[i] = terms(pl.multiple_of(core * half + at, chunk))
+
+        @pl.when(i > 0)
+        def _():
+            pair_sum(i - 1)
+
+    pair_sum(CHUNKS - 1)
+
+    for direction in range(2):
+        for a in range(4):
+            ring_arrival(1, direction, 0, a).wait_recv()
+            share(1, 1 if direction == 0 else chips - 1, a).start()
+
+    @pl.loop(3, chips - 2)
+    def _(k):
+        crossed(k)
+
+    all_shared(1, 0)
+    all_shared(1, 1)
 
     @pl.loop(0, steps)
     def _(s):
-        forward(1, s)
+        gate, up = before(1, s)
+        after(1, s, gate, up)
 
     def take_part(block):
         out = block[:part]
@@ -354,43 +401,55 @@
     def _(s):
         wg_ref[s] = blocks[slots_ref[s]]
 
-    @pl.loop(1, chips)
-    def _(r):
-        spread_sum(r).wait_recv()
-
-    total = acc[pl.ds(pl.multiple_of(chip * chip_rows, chip_rows), chip_rows), :]
-    for r in range(1, chips):
-        total = total + a2a[r].astype(F32)
-    total = total.astype(BF16)
-    low, high = total[:rows], total[rows:]
-    fin_out[...] = jnp.where(core == 0, high, low)
+    mine = pl.ds(pl.multiple_of(chip * chip_rows, chip_rows), chip_rows)
+
+    @pl.loop(0, CHUNKS)
+    def _(i):
+        total = acc[i, mine, :]
+        for r in range(1, chips):
+            spread_sum(r, i).wait_recv()
+            total = total + a2a[i, r].astype(F32)
+        total = total.astype(BF16)
+        low, high = total[:rows], total[rows:]
+        at = pl.multiple_of(i * chunk, chunk)
+        fin_out[:, pl.ds(at, chunk)] = jnp.where(core == 0, high, low)
+        in_ref[:, pl.ds(pl.multiple_of(core * half + at, chunk), chunk)] = jnp.where(core == 0, low, high)
+
     fin = pltpu.make_async_remote_copy(
         src_ref=fin_out, dst_ref=fin_in, send_sem=fin_send, recv_sem=fin_recv,
         device_id=(dp, sibling), device_id_type=MESH,
     )
     fin.start()
-    in_ref[:, pl.ds(pl.multiple_of(core * half, half), half)] = jnp.where(core == 0, low, high)
+
+    @pl.loop(0, CHUNKS)
+    def _(i):
+        to_sibling(i).wait_send()
+
+        @pl.loop(1, chips)
+        def _(r):
+            spread_sum(r, i).wait_send()
+
+    for a in range(4):
+        @pl.loop(0, chips)
+        def _(k):
+            share(0, k, a).wait_send()
+            share(1, k, a).wait_send()
+
+        cross(0, a).wait_send()
+
+        @pl.loop(2, chips - 1)
+        def _(k):
+            cross(k, a).wait_send()
+
+        for direction in range(2):
+            @pl.loop(0, steps if a % 2 == direction else steps - 1)
+            def _(s):
+                ring(0, direction, s, a).wait_send()
+
+            ring(1, direction, 0, a).wait_send()
+
     fin.wait()
     in_ref[:, pl.ds(pl.multiple_of((1 - core) * half, half), half)] = fin_in[...]
-
-    to_sibling.wait_send()
-
-    @pl.loop(1, chips)
-    def _(r):
-        spread_sum(r).wait_send()
-
-    for a in range(2):
-        cross(a).wait_send()
-    for g in range(2):
-        for a in range(2):
-            for direction in range(2):
-                @pl.loop(0, steps if a == direction else steps - 1)
-                def _(s):
-                    ring(g, direction, s, a).wait_send()
-
-            @pl.loop(0, chips)
-            def _(k):
-                share(g, k, a, core).wait_send()
 
 
 def kernel_shards(n_cols, tokens, cotangent, block_weights, slot_block, slot_target, counts):
@@ -430,19 +489,21 @@
             pltpu.VMEM((hidden, features), BF16),
             pltpu.VMEM((n_dp, group_rows, 2 * hidden), BF16),
             pltpu.VMEM((n_dp, group_rows, hidden), BF16),
-            pltpu.VMEM((group_rows, half), F32),
-            pltpu.VMEM((group_rows, half), BF16),
-            pltpu.VMEM((group_rows, half), BF16),
-            pltpu.VMEM((chips, group_rows // chips, half), BF16),
-            pltpu.VMEM((chips, group_rows // chips, half), BF16),
+            pltpu.VMEM((chips // 2, 2, group_rows, hidden // (chips // 2)), F32),
+            pltpu.VMEM((CHUNKS, group_rows, half // CHUNKS), F32),
+            pltpu.VMEM((CHUNKS, group_rows, half // CHUNKS), BF16),
+            pltpu.VMEM((CHUNKS, group_rows, half // CHUNKS), BF16),
+            pltpu.VMEM((CHUNKS, chips, group_rows // chips, half // CHUNKS), BF16),
+            pltpu.VMEM((CHUNKS, chips, group_rows // chips, half // CHUNKS), BF16),
             pltpu.VMEM((rows, half), BF16),
             pltpu.VMEM((rows, half), BF16),
             pltpu.VMEM((4 * part, n_dp * group_rows), BF16),
             pltpu.VMEM((hidden // n_dp, n_dp * group_rows), BF16),
             dma, dma((2,)),
-            dma((2, 2, chips // 2, 2)), dma((2, 2, chips // 2, 2)),
-            dma((2, chips, 2)), dma((2, chips, 2)),
-            dma((2,)), dma((2,)), dma, dma, dma((chips,)), dma((chips,)), dma, dma,
+            dma((2, 2, chips // 2, 4)), dma((2, 2, chips // 2, 4)),
+            dma((2, chips, 4)), dma((2, chips, 4)),
+            dma((chips, 4)), dma((chips, 4)), dma((CHUNKS,)), dma((CHUNKS,)),
+            dma((CHUNKS, chips)), dma((CHUNKS, chips)), dma, dma,
         ],
         compiler_params=pltpu.CompilerParams(
             collective_id=0, has_side_effects=True, vmem_limit_bytes=67043328

time: 97.6 us -> 83.8 us (0.86)
  the two profiles are of different devices: /device:TPU:13 before, /device:TPU:0 now
where the time goes in v2:
time: 83.8 us; the launch traced here: 83.5 us
  Pallas kernels  73.4 us (88%)
  local copies, waits for them, and re-layouts  6.73 us (8%)
  other arithmetic  2.1 us (3%)
  between operations  1.3 us (2%)
    pallas_call x1, Pallas kernels, kernel_shards(): pl.pallas_call(functools.partial(layer_kernel, n_cols), out_shape=(jax.Sh...  73.4 us
    unnamed x2, local copies, waits for them, and re-layouts  6.73 us

profile of v2, /device:TPU:0, one launch (start us, length us, event | category | flops | bytes accessed | tf_op | source)
XLA Modules:
  0.0 83.5 jit_solution(1911802510790735369)
XLA Ops:
  1.3 1.3 %broadcast_select_fusion = (s32[256]{0:T(256)}, s32[256]{0:T(256)S(1)}, s32[256]{0:T(256)S(1)}) fusion(s32[]{:T(128)} %bitcast.3, s32[256]{0:T(256)} %param.9, s32[256]{0:T(256)} %param.10), kind=kLoop, calls=%fused_computation.7 | loop fusion | flops 1280 | bytes 5124 | tf_op jit(solution)/shard_map/jit(_where)/select_n | solution.py:469
  2.6 0.2 select_reduce_fusion
  2.8 0.6 broadcast_add_fusion.table_ref
  3.4 73.4 %shard_map.77 = (bf16[16,4096]{1,0:T(8,128)(2,1)}, bf16[256,64,128]{2,1,0:T(8,128)(2,1)}) custom-call(s32[768]{0:T(1024)} %broadcast_add_fusion.table_ref, s32[256]{0:T(256)} %get-tuple-element.2.slots_ref, bf16[16,4096]{1,0:T(8,128)(2,1)} %tok_ref.1, bf16[16,4096]{1,0:T(8,128)(2,1)} %cot_ref.1, bf16[512,64,128]{2,1,0:T(8,128)(2,1)} %bitcast.4), custom_call_target="tpu_custom_call" | custom-call | tf_op jit(solution)/shard_map/pallas_call | solution.py:476
  76.8 1.6 %copy.11 = bf16[16,4096]{1,0:T(8,128)(2,1)} copy(bf16[16,4096]{1,0:T(8,128)(2,1)} %get-tuple-element.7) | data formatting | bytes 262144
  78.4 5.2 %copy.12 = bf16[256,64,128]{2,1,0:T(8,128)(2,1)} copy(bf16[256,64,128]{2,1,0:T(8,128)(2,1)} %get-tuple-element.8) | data formatting | bytes 8388608
  (1 shorter events, 0.0 us)

commit v3 on v2

--- a/solution.py
+++ b/solution.py
@@ -121,15 +121,17 @@
     sibling = chip * 2 + 1 - core
     sides = ((tok_ref, tok), (cot_ref, cot))
 
+    owns = [pltpu.make_async_copy(sides[a][0], sides[a][1].at[0, col], own_sem.at[a]) for a in range(2)]
+    for own in owns:
+        own.start()
+    w_copy = pltpu.make_async_copy(w_ref, blocks.at[pl.ds(0, w_ref.shape[0])], w_sem)
+    w_copy.start()
     barrier = pltpu.get_barrier_semaphore()
     for r in range(1, chips):
         pl.semaphore_signal(barrier, inc=1, device_id=(dp, ((chip + r) % chips) * 2 + core), device_id_type=MESH)
     pl.semaphore_signal(barrier, inc=1, device_id=(dp, sibling), device_id_type=MESH)
     pl.semaphore_signal(barrier, inc=1, device_id=(1 - dp, col), device_id_type=MESH)
     pl.semaphore_wait(barrier, chips + 1)
-
-    w_copy = pltpu.make_async_copy(w_ref, blocks.at[pl.ds(0, w_ref.shape[0])], w_sem)
-    w_copy.start()
 
     def piece(g, origin, a):
         at = pl.ds((a % 2) * half, half)
@@ -214,9 +216,7 @@
             cross(k, a).wait_recv()
             share(1, k, a).start()
 
-    for a in range(2):
-        own = pltpu.make_async_copy(sides[a][0], sides[a][1].at[0, col], own_sem.at[a])
-        own.start()
+    for own in owns:
         own.wait()
     first(0, 0)
     blocks[zero_at] = jnp.zeros((part, width), BF16)
@@ -409,7 +409,6 @@
         for r in range(1, chips):
             spread_sum(r, i).wait_recv()
             total = total + a2a[i, r].astype(F32)
-        total = total.astype(BF16)
         low, high = total[:rows], total[rows:]
         at = pl.multiple_of(i * chunk, chunk)
         fin_out[:, pl.ds(at, chunk)] = jnp.where(core == 0, high, low)
@@ -466,17 +465,17 @@
     live = number < counts[0]
     hit = (place[None, :] == jnp.arange(places, dtype=jnp.int32)[:, None]) & live[None, :]
     table = places + jnp.sum(jnp.where(hit, number[None, :] - places, 0), axis=1)
-    slots = jnp.where(live, place, places)
+    slots = jnp.where(live, place, 0)
     chips = n_cols // 2
     group_rows = rows * n_cols
     half = features // 2
     dma = pltpu.SemaphoreType.DMA
     vmem = pl.BlockSpec(memory_space=pltpu.VMEM)
     smem = pl.BlockSpec(memory_space=pltpu.SMEM)
-    return pl.pallas_call(
+    input_sum, weight_sum = pl.pallas_call(
         functools.partial(layer_kernel, n_cols),
         out_shape=(
-            jax.ShapeDtypeStruct((rows, features), BF16),
+            jax.ShapeDtypeStruct((rows, features), F32),
             jax.ShapeDtypeStruct((n_slots, part, width), BF16),
         ),
         in_specs=[smem, smem, vmem, vmem, pl.BlockSpec(memory_space=pl.ANY)],
@@ -495,8 +494,8 @@
             pltpu.VMEM((CHUNKS, group_rows, half // CHUNKS), BF16),
             pltpu.VMEM((CHUNKS, chips, group_rows // chips, half // CHUNKS), BF16),
             pltpu.VMEM((CHUNKS, chips, group_rows // chips, half // CHUNKS), BF16),
-            pltpu.VMEM((rows, half), BF16),
-            pltpu.VMEM((rows, half), BF16),
+            pltpu.VMEM((rows, half), F32),
+            pltpu.VMEM((rows, half), F32),
             pltpu.VMEM((4 * part, n_dp * group_rows), BF16),
             pltpu.VMEM((hidden // n_dp, n_dp * group_rows), BF16),
             dma, dma((2,)),
@@ -509,6 +508,8 @@
             collective_id=0, has_side_effects=True, vmem_limit_bytes=67043328
         ),
     )(table, slots, tokens, cotangent, block_weights.reshape(n_slots * n_dp, part, width))
+    weight_grad = jnp.where(live[:, None, None], weight_sum, jnp.zeros((), BF16))
+    return (input_sum.astype(BF16), weight_grad)
 
 
 def solution(mesh):

time: 83.8 us -> 81.5 us (0.973)
  local copies, waits for them, and re-layouts: 6.73 us -> 0.01 us
  other arithmetic: 2.1 us -> 7.71 us
  Pallas kernels: 73.4 us -> 72.2 us
    unnamed x2, local copies, waits for them, and re-layouts: 6.73 us -> 0.01 us
    select_n x1 -> x2, other arithmetic: 1.26 us -> 5.25 us  [the longest x1 3.99 us: kernel_shards(): jnp.where(live[:, None, None], weight_sum, jnp.zeros((), BF16))]
    convert_element_type x0 -> x1, other arithmetic: none -> 1.62 us  [kernel_shards(): return (input_sum.astype(BF16), weight_grad)]
    pallas_call x1, Pallas kernels: 73.4 us -> 72.2 us  [kernel_shards(): pl.pallas_call(functools.partial(layer_kernel, n_cols), out_shape=(jax.Sh...]
where the time goes in v3:
time: 81.5 us; the launch traced here: 81.3 us
  Pallas kernels  72.2 us (89%)
  other arithmetic  7.71 us (9%)
  between operations  1.31 us (2%)
    pallas_call x1, Pallas kernels, kernel_shards(): pl.pallas_call(functools.partial(layer_kernel, n_cols), out_shape=(jax.Sh...  72.2 us
    select_n x1, other arithmetic, kernel_shards(): jnp.where(live[:, None, None], weight_sum, jnp.zeros((), BF16))  3.99 us

profile of v3, /device:TPU:0, one launch (start us, length us, event | category | flops | bytes accessed | tf_op | source)
XLA Modules:
  0.0 81.3 jit_solution(2344352274056538426)
XLA Ops:
  1.3 0.0 copy-start
  1.3 1.3 %broadcast_select_fusion.1 = (s32[256]{0:T(256)}, s32[256]{0:T(256)S(1)}, s32[256]{0:T(256)S(1)}) fusion(s32[]{:T(128)} %bitcast.3, s32[256]{0:T(256)} %param.9, s32[256]{0:T(256)} %param.10), kind=kLoop, calls=%fused_computation.8 | loop fusion | flops 1280 | bytes 5124 | tf_op jit(solution)/shard_map/jit(_where)/select_n | solution.py:468
  2.6 0.2 select_reduce_fusion
  2.8 0.0 copy-done
  2.8 0.6 broadcast_add_fusion.table_ref
  3.4 72.2 %shard_map.77 = (f32[16,4096]{1,0:T(8,128)}, bf16[256,64,128]{2,1,0:T(8,128)(2,1)}) custom-call(s32[768]{0:T(1024)} %broadcast_add_fusion.table_ref, s32[256]{0:T(256)} %get-tuple-element.6.slots_ref, bf16[16,4096]{1,0:T(8,128)(2,1)} %tok_ref.1, bf16[16,4096]{1,0:T(8,128)(2,1)} %cot_ref.1, bf16[512,64,128]{2,1,0:T(8,128)(2,1)} %bitcast.4), custom_call_target="tpu_custom_call" | custom-call | tf_op jit(solution)/shard_map/pallas_call | solution.py:475
  75.6 1.6 %convert_element_type.3 = bf16[16,4096]{1,0:T(8,128)(2,1)} convert(f32[16,4096]{1,0:T(8,128)} %get-tuple-element.4) | non-fusion elementwise | flops 65536 | bytes 393216 | tf_op jit(solution)/shard_map/convert_element_type | solution.py:512
  77.3 4.0 %broadcast_select_fusion = bf16[256,64,128]{2,1,0:T(8,128)(2,1)} fusion(bf16[256,64,128]{2,1,0:T(8,128)(2,1)} %get-tuple-element.5, pred[256]{0:T(512)(128)(4,1)} %copy-done), kind=kLoop, calls=%fused_computation | loop fusion | flops 2097152 | bytes 8388864 | tf_op jit(solution)/shard_map/jit(_where)/select_n | solution.py:511
  (1 shorter events, 0.0 us)
Async XLA Ops:
  1.3 1.5 %copy-start = (pred[256]{0:T(512)(128)(4,1)}, pred[256]{0:T(512)(128)(4,1)S(1)}, u32[]{:S(2)}) copy-start(pred[256]{0:T(512)(128)(4,1)S(1)} %iota_compare_fusion.1) | copy-start | bytes 772
